TPU v7x, 32 devices: a whole 2x2x4 slice. The times are simulated.
32 devices in a mesh: survey: 2 (over x), chan: 16 (over z, y, core).
Axes of the slice: x: 2, y: 2, z: 4, core: 2. Of those that a mesh axis runs over, the one named last changes fastest.
Arguments:
- das_window: float32 [8192, 8192], P(('survey', 'chan')), parts along dimension 0, may hold values from -6 to 6
- fan_bound: int32 [4096], replicated, may hold values from -1 to 2048, as said below
- tap_offset: int32 [8, 32], replicated, may hold values from -31 to 31, as said below
- tap_weight: float32 [8, 32], replicated, may hold values from -1 to 1
Outputs:
- filtered: float32 [8192, 8192], P(('survey', 'chan')), parts along dimension 0
- energy: float32 [8192, 8, 128], P(('survey', 'chan')), parts along dimension 0
There are 2 independent parts, one for each index of `survey`. A program takes and returns all parts, laid end to end along the dimension named above; an argument that names none is the same for every part. Nothing has to cross between parts.
Inputs may be any that keep to these rules, and one draw needn't show every extreme that they name: `fan_bound`: entry f bounds the magnitude of the signed channel wavenumber bin passed at the time frequency bins +f and -f; -1 passes none. `tap_offset`: the channel offset of a tap relative to the output channel.
All inputs are finite; a program needn't handle non-finite values.
Results may differ from a plain program's by a relative error of at most 0.0027.
Values may be sent and summed in bfloat16 or wider, within the bound.
No kernel may reach another device: no remote copies, remote signals or barrier semaphores. Data moves between devices by JAX's collectives and lax.ppermute only.
A program may use at most 256 MiB of HBM per device.

v0:
```python
import math

import jax
import jax.numpy as jnp
from jax import lax
from jax.sharding import PartitionSpec as P

HALO = 31
WIN = 64


PRECISE = lax.Precision.HIGHEST


def padded_2(value, sides, width):
    for axis, dim in sides:
        peers, length = (lax.axis_size(axis), value.shape[dim])
        up = [(i, (i + 1) % peers) for i in range(peers - 1)]
        down = [(j, i) for i, j in up]
        last = lax.slice_in_dim(value, length - width, length, axis=dim)
        leading = lax.slice_in_dim(value, 0, width, axis=dim)
        before = lax.ppermute(last, axis, up)
        after = lax.ppermute(leading, axis, down)
        value = jnp.concatenate([before, value, after], axis=dim)
    return value


def split_length(length_all):
    leading = 1
    while length_all % (4 * leading) == 0 and 4 * leading * leading <= length_all:
        leading = leading * 2
    return (leading, length_all // leading)


def phases(index_product, modulus, direction):
    angle = (index_product % modulus).astype(jnp.float32) * (2.0 * math.pi / modulus)
    return (jnp.cos(angle), direction * jnp.sin(angle))


def complex_table(real_part, imag_part, q_axis):
    first_row = jnp.stack([real_part, imag_part], axis=q_axis)
    second_row = jnp.stack([-imag_part, real_part], axis=q_axis)
    return jnp.stack([first_row, second_row], axis=0)


def square_phases(leading, direction):
    left_index = lax.broadcasted_iota(jnp.int32, (leading, leading), 0)
    right_index = lax.broadcasted_iota(jnp.int32, (leading, leading), 1)
    return phases(left_index * right_index, leading, direction)


def folded_table(shape_three, bin_axis, inner_axis, leading, modulus, direction):
    bin_index = lax.broadcasted_iota(jnp.int32, shape_three, bin_axis)
    outer_index = lax.broadcasted_iota(jnp.int32, shape_three, 3 - bin_axis - inner_axis)
    inner_index = lax.broadcasted_iota(jnp.int32, shape_three, inner_axis)
    return phases(inner_index * (bin_index + leading * outer_index), modulus, direction)


def time_forward(signal, kept_bins):
    row_count, sample_count = signal.shape
    leading, trailing = split_length(sample_count)
    used_bins = kept_bins // leading
    shaped = signal.reshape(row_count, leading, trailing)
    cos_first, sin_first = square_phases(leading, -1.0)
    first_table = jnp.stack([cos_first, sin_first], axis=1)
    first = jnp.einsum("rab,apk->rpkb", shaped, first_table, precision=PRECISE)
    cos_second, sin_second = folded_table(
        (leading, trailing, used_bins), 0, 1, leading, sample_count, -1.0
    )
    second_table = complex_table(cos_second, sin_second, 2)
    out = jnp.einsum("rpkb,pkbqm->rqmk", first, second_table, precision=PRECISE)
    return out.reshape(row_count, 2, kept_bins)


def channel_transform(field, direction):
    length_all, parts_count, column_count = field.shape
    leading, trailing = split_length(length_all)
    shaped = field.reshape(leading, trailing, parts_count, column_count)
    cos_first, sin_first = square_phases(leading, direction)
    first_table = complex_table(cos_first, sin_first, 1)
    first = jnp.einsum("abpn,paqk->kbqn", shaped, first_table, precision=PRECISE)
    cos_second, sin_second = folded_table(
        (leading, trailing, trailing), 0, 1, leading, length_all, direction
    )
    second_table = complex_table(cos_second, sin_second, 2)
    out = jnp.einsum("kbpn,pkbqm->mkqn", first, second_table, precision=PRECISE)
    return out.reshape(length_all, parts_count, column_count)


def time_inverse(spectrum, sample_count):
    row_count, parts_count, bin_count = spectrum.shape
    leading, trailing = split_length(sample_count)
    used_bins = bin_count // leading
    shaped = spectrum.reshape(row_count, parts_count, used_bins, leading)
    cos_first, sin_first = folded_table(
        (leading, used_bins, trailing), 0, 2, leading, sample_count, 1.0
    )
    first_table = complex_table(cos_first, sin_first, 2)
    first = jnp.einsum("rpmk,pkmqb->rqkb", shaped, first_table, precision=PRECISE)
    cos_last, sin_last = square_phases(leading, 1.0)
    last_table = jnp.stack([cos_last, -sin_last], axis=0)
    signal = jnp.einsum("rqkb,qka->rab", first, last_table, precision=PRECISE)
    signal = signal.reshape(row_count, sample_count)
    signal = 2.0 * signal - spectrum[:, 0, 0:1]
    return signal / sample_count


def per_device(das_window, fan_bound, tap_offset, tap_weight):
    row_count, sample_count = das_window.shape
    devices = lax.axis_size("chan")
    channel_count = row_count * devices
    kept_bins = sample_count // 2
    block_bins = kept_bins // devices
    spectrum = time_forward(das_window, kept_bins)
    by_freq = lax.all_to_all(spectrum, "chan", split_axis=2, concat_axis=0, tiled=True)
    wave = channel_transform(by_freq, -1.0)
    wave_index = lax.broadcasted_iota(jnp.int32, (channel_count, 1), 0)
    wave_signed = jnp.where(wave_index < channel_count // 2, wave_index, wave_index - channel_count)
    position = lax.axis_index("chan")
    extended = jnp.concatenate([fan_bound, jnp.full((1,), -1, jnp.int32)])
    limits = lax.dynamic_slice_in_dim(extended, position * block_bins, block_bins)
    passing = (jnp.abs(wave_signed) <= limits[None, :]).astype(jnp.float32)
    back = channel_transform(wave * passing[:, None, :], 1.0) / channel_count
    by_channel = lax.all_to_all(back, "chan", split_axis=0, concat_axis=2, tiled=True)
    filtered = time_inverse(by_channel, sample_count)
    low_field = filtered.astype(jnp.bfloat16)
    padded = padded_2(low_field, (("chan", 0),), HALO)
    span_count = 2 * HALO + 1
    offsets_grid = jnp.arange(span_count, dtype=jnp.int32) - HALO
    matches = (tap_offset[:, :, None] == offsets_grid[None, None, :]).astype(jnp.float32)
    kernel_low = jnp.sum(tap_weight[:, :, None] * matches, axis=1).astype(jnp.bfloat16)
    template_count = kernel_low.shape[0]
    piece_rows = 64
    offset_index = lax.broadcasted_iota(
        jnp.int32, (span_count, piece_rows, piece_rows + 2 * HALO), 0
    )
    output_index = lax.broadcasted_iota(
        jnp.int32, (span_count, piece_rows, piece_rows + 2 * HALO), 1
    )
    input_index = lax.broadcasted_iota(
        jnp.int32, (span_count, piece_rows, piece_rows + 2 * HALO), 2
    )
    selector = (input_index - output_index == offset_index).astype(jnp.bfloat16)
    stacking = jnp.einsum("ko,ori->rki", kernel_low, selector, preferred_element_type=jnp.float32)
    stacking = stacking.astype(jnp.bfloat16).reshape(
        piece_rows * template_count, piece_rows + 2 * HALO
    )

    def one_piece(first_row):
        window_rows = lax.dynamic_slice_in_dim(padded, first_row, piece_rows + 2 * HALO, 0)
        detection = jnp.dot(stacking, window_rows, preferred_element_type=jnp.float32)
        squared = (detection * detection).reshape(
            piece_rows * template_count, sample_count // WIN, WIN
        )
        return jnp.mean(squared, axis=2).reshape(piece_rows, template_count, sample_count // WIN)

    starts = jnp.arange(0, row_count, piece_rows, dtype=jnp.int32)
    energy = lax.map(one_piece, starts).reshape(row_count, template_count, sample_count // WIN)
    return (filtered, energy)


def solution(mesh):
    return jax.shard_map(
        per_device,
        mesh=mesh,
        in_specs=(P(("survey", "chan"), None), P(), P(), P()),
        out_specs=(P(("survey", "chan"), None), P(("survey", "chan"), None, None)),
        check_vma=False,
    )
```

profile of v0, /device:TPU:17, one launch (start us, length us, event | category | flops | bytes accessed | tf_op | source)
XLA Modules:
  0.0 740.6 jit_solution(12700331765586824724)
XLA Ops:
  0.6 0.1 broadcast_multiply_fusion.2
  0.8 8.4 %sine_multiply_fusion = (f32[64,128,1,64]{1,3,2,0:T(8,128)S(1)}, f32[64,128,1,64]{1,3,2,0:T(8,128)S(1)}, f32[64,128,1,64]{1,3,2,0:T(8,128)S(1)}) fusion(s32[64]{0:T(128)S(1)} %iota_multiply_fusion.1), kind=kLoop, calls=%fused_computation.74 | loop fusion | flops 8912896 | bytes 6291712 | tf_op jit(solution)/shard_map/mul | solution.py:37
  9.2 5.0 copy.102
  14.3 4.3 maximum_bitcast_fusion.2
  18.6 16.0 %convolution_bitcast_fusion.1 = f32[256,2,64,128,1]{3,2,0,1,4:T(8,128)} fusion(f32[256,64,128,1]{2,1,0,3:T(8,128)S(1)} %bitcast.148, f32[64,1,64]{0,2,1:T(8,128)S(1)} %get-tuple-element.68, f32[64,1,64]{0,2,1:T(8,128)S(1)} %get-tuple-element.67), kind=kOutput, calls=%fused_computation.37 | convolution fusion | flops 3221233664 | bytes 25198592 | tf_op jit(solution)/shard_map/rab,apk->rpkb/dot_general | solution.py:66
  34.6 33.7 %fusion.37 = f32[256,2,64,64]{0,2,1,3:T(8,128)S(1)} fusion(f32[256,2,64,128,1]{3,2,0,1,4:T(8,128)} %convolution_bitcast_fusion.1, f32[1,64,128,2,64]{2,4,0,3,1:T(8,128)} %get-tuple-element.51, f32[1,64,128,2,64]{2,4,0,3,1:T(8,128)} %get-tuple-element.50), kind=kOutput, calls=%fused_computation.54 | convolution fusion | flops 6444548096 | bytes 33554432 | tf_op jit(solution)/shard_map/rpkb,pkbqm->rqmk/dot_general | solution.py:71
  68.3 4.9 copy.56
  73.1 23.4 %copy.57 = f32[256,2,4096]{0,1,2:T(2,128)} copy(f32[256,2,4096]{0,2,1:T(8,128)S(1)} %bitcast.153) | data formatting | bytes 16777216 | tf_op jit(solution)/shard_map/reshape | solution.py:72
  96.6 6.9 all-to-all-start
  103.5 0.1 fusion.92
  103.6 0.1 fusion.89
  103.8 0.1 fusion.85
  104.0 2.3 compare_convert_fusion
  106.3 8.5 %broadcast_multiply_fusion.1 = (f32[64,64,1,64]{1,3,0,2:T(8,128)S(1)}, f32[64,64,1,64]{1,3,0,2:T(8,128)S(1)}, f32[64,64,1,64]{1,3,0,2:T(8,128)S(1)}, f32[64,64,1,64]{1,3,0,2:T(8,128)S(1)}, f32[64,64,1,64]{1,3,0,2:T(8,128)S(1)}) fusion(s32[64]{0:T(128)S(1)} %iota_multiply_fusion.1), kind=kLoop, calls=%fused_computation.83 | loop fusion | flops 4718592 | bytes 5243136 | tf_op jit(solution)/shard_map/mul | solution.py:37
  114.8 7.4 fusion.30
  122.1 163.3 %all-to-all-done = f32[256,2,4096]{0,1,2:T(2,128)} async-done(((f32[256,2,4096]{0,1,2:T(2,128)}), f32[256,2,4096]{0,1,2:T(2,128)}, u32[]{:S(2)}, u32[]{:S(2)}) %all-to-all-start) | async-done | bytes 8388640 | tf_op jit(solution)/shard_map/all_to_all | solution.py:115
  285.4 7.4 %copy.58 = f32[256,2,4096]{0,2,1:T(8,128)} copy(f32[256,2,4096]{0,1,2:T(2,128)} %all-to-all-done) | data formatting | bytes 16777216 | tf_op jit(solution)/shard_map/all_to_all | solution.py:115
  292.9 8.7 %copy.59 = f32[16,256,2,256]{3,1,0,2:T(8,128)} copy(f32[16,256,2,256]{1,3,0,2:T(8,128)} %bitcast.154) | data formatting | bytes 16777216 | tf_op jit(solution)/shard_map/all_to_all | solution.py:115
  301.6 17.6 %fusion.31 = f32[64,64,2,256,1]{3,0,1,2,4:T(8,128)} fusion(f32[64,64,2,256]{3,1,0,2:T(8,128)} %bitcast.152, f32[1,64,2,64]{1,3,2,0:T(8,128)S(1)} %get-tuple-element.53, f32[1,64,2,64]{1,3,2,0:T(8,128)S(1)} %get-tuple-element.54), kind=kOutput, calls=%fused_computation.52 | convolution fusion | flops 3221241856 | bytes 16842752 | tf_op jit(solution)/shard_map/abpn,paqk->kbqn/dot_general | solution.py:81
  319.2 22.0 %fusion.20 = f32[64,2,64,256,1]{3,2,1,0,4:T(8,128)} fusion(f32[64,64,2,256,1]{3,0,1,2,4:T(8,128)} %fusion.31, f32[1,64,64,2,64]{2,4,1,3,0:T(8,128)} %get-tuple-element.47, f32[1,64,64,2,64]{2,4,1,3,0:T(8,128)} %get-tuple-element.46), kind=kOutput, calls=%fused_computation.30 | convolution fusion | flops 3222274048 | bytes 20971520 | tf_op jit(solution)/shard_map/kbpn,pkbqm->mkqn/dot_general | solution.py:86
  341.3 11.9 %fusion.34 = f32[64,64,2,256,1]{3,0,1,2,4:T(8,128)} fusion(f32[64,2,64,256,1]{3,2,1,0,4:T(8,128)} %fusion.20, f32[64,64,256]{2,0,1:T(8,128)S(1)} %copy-done.1, f32[1,64,2,64]{1,3,2,0:T(8,128)S(1)} %get-tuple-element.55, f32[1,64,2,64]{1,3,2,0:T(8,128)S(1)} %get-tuple-element.52), kind=kOutput, calls=%fused_computation.53 | convolution fusion | flops 3223339008 | bytes 21037056 | tf_op jit(solution)/shard_map/abpn,paqk->kbqn/dot_general | solution.py:81
  353.2 22.1 %fusion.8 = f32[64,2,64,256,1]{3,2,0,1,4:T(8,128)} fusion(f32[1,64,64,2,64]{2,4,1,3,0:T(8,128)} %get-tuple-element.48, f32[1,64,64,2,64]{2,4,1,3,0:T(8,128)} %get-tuple-element.49, f32[64,64,2,256,1]{3,0,1,2,4:T(8,128)} %fusion.34), kind=kOutput, calls=%fused_computation.14 | convolution fusion | flops 3222274048 | bytes 20971520 | tf_op jit(solution)/shard_map/kbpn,pkbqm->mkqn/dot_general | solution.py:86
  375.3 4.3 fusion.16
  379.6 4.9 copy.67
  384.4 23.4 %copy.68 = f32[4096,2,256]{2,1,0:T(2,128)} copy(f32[4096,2,256]{2,0,1:T(8,128)S(1)} %bitcast.155) | data formatting | bytes 16777216 | tf_op jit(solution)/shard_map/div | solution.py:123
  407.9 5.2 all-to-all-start.1
  413.1 0.1 sine_negate_fusion
  413.2 8.4 %fusion.55 = (f32[64,64,1,128]{3,1,2,0:T(8,128)S(1)}, f32[64,64,1,128]{3,1,2,0:T(8,128)S(1)}, f32[64,64,1,128]{3,1,2,0:T(8,128)S(1)}) fusion(s32[64]{0:T(128)S(1)} %iota_multiply_fusion.1), kind=kLoop, calls=%fused_computation.79 | loop fusion | flops 8388608 | bytes 6291712 | tf_op jit(solution)/shard_map/sin | solution.py:37
  421.7 4.2 maximum_bitcast_fusion
  425.9 169.3 %all-to-all-done.1 = f32[4096,2,256]{2,1,0:T(2,128)} async-done(((f32[4096,2,256]{2,1,0:T(2,128)}), f32[4096,2,256]{2,1,0:T(2,128)}, u32[]{:S(2)}, u32[]{:S(2)}) %all-to-all-start.1) | async-done | bytes 8388640 | tf_op jit(solution)/shard_map/all_to_all | solution.py:124
  595.2 7.4 %copy.69 = f32[4096,2,256]{2,0,1:T(8,128)} copy(f32[4096,2,256]{2,1,0:T(2,128)} %all-to-all-done.1) | data formatting | bytes 16777216 | tf_op jit(solution)/shard_map/all_to_all | solution.py:124
  602.6 8.7 %copy.70 = f32[256,2,16,256]{0,3,2,1:T(8,128)} copy(f32[256,2,16,256]{3,0,2,1:T(8,128)} %bitcast.156) | data formatting | bytes 16777216 | tf_op jit(solution)/shard_map/all_to_all | solution.py:124
  611.3 31.8 %convolution_bitcast_fusion = f32[256,2,64,128]{0,3,1,2:T(8,128)} fusion(f32[1,64,64,2,128]{4,2,0,3,1:T(8,128)} %get-tuple-element.45, f32[1,64,64,2,128]{4,2,0,3,1:T(8,128)} %get-tuple-element.44, f32[256,2,64,64,1]{0,3,2,1,4:T(8,128)} %bitcast.149), kind=kOutput, calls=%fused_computation.8 | convolution fusion | flops 6444548096 | bytes 33554432 | tf_op jit(solution)/shard_map/rpmk,pkmqb->rqkb/dot_general | solution.py:99
  643.1 16.8 %copy.72 = f32[256,2,64,128]{3,2,1,0:T(8,128)} copy(f32[256,2,64,128]{0,3,1,2:T(8,128)} %convolution_bitcast_fusion) | data formatting | bytes 33554432 | tf_op jit(solution)/shard_map/rpmk,pkmqb->rqkb/transpose | solution.py:99
  659.9 0.7 slice.12
  660.6 12.2 %bitcast_multiply_fusion.1 = f32[64,256,128]{2,0,1:T(8,128)S(1)} fusion(f32[256,2,64,128]{3,2,1,0:T(8,128)} %copy.72, f32[1,64,64]{1,2,0:T(8,128)S(1)} %get-tuple-element.71, f32[1,64,64]{1,2,0:T(8,128)S(1)} %get-tuple-element.72), kind=kOutput, calls=%fused_computation.23 | convolution fusion | flops 3223330816 | bytes 25198592 | tf_op jit(solution)/shard_map/rqkb,qka->rab/dot_general | solution.py:102
  672.8 0.0 copy-start.3
  672.8 11.9 %fusion.98 = (bf16[256,8192]{1,0:T(8,128)(2,1)S(1)}, f32[256,8192]{1,0:T(8,128)}) fusion(f32[256]{0:T(256)S(1)} %bitcast.158, f32[32,8,64,128]{3,2,1,0:T(8,128)S(1)} %bitcast.151), kind=kLoop, calls=%fused_computation.144 | loop fusion | flops 6291456 | bytes 20972544 | tf_op jit(solution)/shard_map/convert_element_type | solution.py:126
  684.7 2.0 copy-done
  686.7 0.1 fusion.100
  686.8 2.0 collective-permute-start
  688.9 2.7 collective-permute-start.1
  691.6 0.1 select_reduce_fusion
  691.8 0.5 fusion.58
  692.2 8.4 %collective-permute-done = bf16[31,8192]{1,0:T(8,128)(2,1)S(1)} collective-permute-done((bf16[31,8192]{1,0:T(8,128)(2,1)S(1)}, bf16[31,8192]{1,0:T(8,128)(2,1)S(1)}, u32[]{:S(2)}, u32[]{:S(2)}) %collective-permute-start) | collective-permute-done | bytes 507936 | tf_op jit(solution)/shard_map/ppermute | solution.py:22
  700.6 3.4 collective-permute-done.1
  704.0 6.4 pad_maximum_fusion.1
  710.4 29.7 %while.10 = (s32[]{:T(128)}, f32[4,64,8,128]{3,2,1,0:T(8,128)}, s32[4]{0:T(128)S(1)}, bf16[318,8192]{1,0:T(8,128)(2,1)}, bf16[512,126]{1,0:T(8,128)(2,1)S(1)}, /*index=5*/s32[]{:T(128)}, s32[]{:T(128)}, s32[]{:T(128)}) while((s32[]{:T(128)}, f32[4,64,8,128]{3,2,1,0:T(8,128)}, s32[4]{0:T(128)S(1)}, bf16[318,8192]{1,0:T(8,128)(2,1)}, ...), condition=%wide.region_3.4_spmd, body=%wide.region_1.3_spmd.sunk | while | flops 1065353216 | bytes 4061831 | solution.py:158
  710.4 0.6 dynamic_slice.22
  712.9 4.0 bitcast_reduce_fusion.2
  717.0 0.1 copy.139
  717.1 0.7 bitcast_dynamic-update-slice_fusion.2
  717.9 0.6 dynamic_slice.22
  720.4 4.1 bitcast_reduce_fusion.2
  724.5 0.1 copy.139
  724.6 0.7 bitcast_dynamic-update-slice_fusion.2
  725.3 0.6 dynamic_slice.22
  727.8 4.0 bitcast_reduce_fusion.2
  731.9 0.1 copy.139
  732.0 0.7 bitcast_dynamic-update-slice_fusion.2
  732.7 0.6 dynamic_slice.22
  735.2 4.0 bitcast_reduce_fusion.2
  739.3 0.1 copy.139
  739.4 0.7 bitcast_dynamic-update-slice_fusion.2
  (18 shorter events, 0.2 us)
Async XLA Ops:
  96.6 7.0 copy-start.2
  96.6 188.8 %all-to-all-start = ((f32[256,2,4096]{0,1,2:T(2,128)}), f32[256,2,4096]{0,1,2:T(2,128)}, u32[]{:S(2)}, u32[]{:S(2)}) async-start(f32[256,2,4096]{0,1,2:T(2,128)} %copy.57), calls=%async_computation | async-start | bytes 16777216 | tf_op jit(solution)/shard_map/all_to_all | solution.py:115
  319.2 22.1 %copy-start.1 = (f32[64,64,256]{2,0,1:T(8,128)S(1)}, f32[64,64,256]{2,0,1:T(8,128)}, u32[]{:S(2)}) copy-start(f32[64,64,256]{2,0,1:T(8,128)} %compare_convert_fusion) | copy-start | bytes 12582916
  407.9 187.3 %all-to-all-start.1 = ((f32[4096,2,256]{2,1,0:T(2,128)}), f32[4096,2,256]{2,1,0:T(2,128)}, u32[]{:S(2)}, u32[]{:S(2)}) async-start(f32[4096,2,256]{2,1,0:T(2,128)} %copy.68), calls=%async_computation.1 | async-start | bytes 16777216 | tf_op jit(solution)/shard_map/all_to_all | solution.py:124
  672.8 18.8 %copy-start.3 = (f32[8,32]{1,0:T(8,128)S(1)}, f32[8,32]{1,0:T(8,128)}, u32[]{:S(2)}) copy-start(f32[8,32]{1,0:T(8,128)} %param.9) | copy-start | bytes 3076
  672.8 18.8 %copy-start.4 = (s32[8,32]{1,0:T(8,128)S(1)}, s32[8,32]{1,0:T(8,128)}, u32[]{:S(2)}) copy-start(s32[8,32]{1,0:T(8,128)} %param.8) | copy-start | bytes 3076
  684.7 2.0 copy-start
  686.8 13.8 %collective-permute-start = (bf16[31,8192]{1,0:T(8,128)(2,1)S(1)}, bf16[31,8192]{1,0:T(8,128)(2,1)S(1)}, u32[]{:S(2)}, u32[]{:S(2)}) collective-permute-start(bf16[31,8192]{1,0:T(8,128)(2,1)S(1)} %get-tuple-element.42), channel_id=1, source_target_pairs={{0,1},{1,2},{2,3},{3,4},{4,5},{5,6},{6,7},{7,8},{8,9},{9,10},{10,1... | collective-permute-start | bytes 1523720 | tf_op jit(solution)/shard_map/ppermute | solution.py:22
  688.9 15.2 %collective-permute-start.1 = (bf16[31,8192]{1,0:T(8,128)(2,1)S(1)}, bf16[31,8192]{1,0:T(8,128)(2,1)S(1)}, u32[]{:S(2)}, u32[]{:S(2)}) collective-permute-start(bf16[31,8192]{1,0:T(8,128)(2,1)S(1)} %get-tuple-element.43), channel_id=1, source_target_pairs={{1,0},{2,1},{3,2},{4,3},{5,4},{6,5},{7,6},{8,7},{9,8},{10,9},{11,1... | collective-permute-start | bytes 1523720 | tf_op jit(solution)/shard_map/ppermute | solution.py:23
where the time goes:
time: 750 us; the launch traced here: 741 us
  waiting for transfers between devices  344 us (46%)
  matrix products  184 us (25%)
  local copies, waits for them, and re-layouts  120 us (16%)
  other arithmetic  67 us (9%)
  starting transfers between devices  16.9 us (2%)
  loops' own time  7.54 us (1%)
    all_to_all x1, waiting for transfers between devices, per_device(): lax.all_to_all(back, 'chan', split_axis=0, concat_axis=2, tiled=True)  169 us
    all_to_all x1, waiting for transfers between devices, per_device(): lax.all_to_all(spectrum, 'chan', split_axis=2, concat_axis=0, tiled=True)  163 us
    dot_general x2, matrix products, channel_transform(): out = jnp.einsum('kbpn,pkbqm->mkqn', first, second_table, precision=PRECISE)  44.2 us
    dot_general x1, matrix products, time_forward(): out = jnp.einsum('rpkb,pkbqm->rqmk', first, second_table, precision=PRECISE)  33.7 us
    dot_general x1, matrix products, time_inverse(): jnp.einsum('rpmk,pkmqb->rqkb', shaped, first_table, precision=PRECISE)  31.8 us
    dot_general x2, matrix products, channel_transform(): jnp.einsum('abpn,paqk->kbqn', shaped, first_table, precision=PRECISE)  29.5 us
    div x2, local copies, waits for them, and re-layouts, per_device(): back = channel_transform(wave * passing[:, None, :], 1.0) / channel_count  28.3 us
    reshape x1, local copies, waits for them, and re-layouts, time_forward(): return out.reshape(row_count, 2, kept_bins)  23.4 us
  transfers between devices with their start and end apart: 4, of which 4 were waited for; matrix products, arithmetic and copies ran while one was open for 4% of the time, Pallas kernels for 0%

commit v1 on v0

v1 whole, which is shorter than its diff:
```python
import functools
import math

import jax
import jax.numpy as jnp
import ml_dtypes
import numpy as np
from jax import lax
from jax.experimental import pallas as pl
from jax.experimental.pallas import tpu as pltpu
from jax.sharding import PartitionSpec as P

HALO = 31
WIN = 64
RADIX = 32
LANES = 256
SLOTS = RADIX // 2
COLS = 2 * LANES
BF = jnp.bfloat16
F32 = jnp.float32


def split_table(table):
    high = table.astype(ml_dtypes.bfloat16)
    low = (table - high.astype(np.float64)).astype(ml_dtypes.bfloat16)
    return np.stack([high, low])


def full_table():
    index = np.arange(LANES)
    angle = 2.0 * np.pi * ((index[:, None] * index[None, :]) % LANES) / LANES
    cos, sin = np.cos(angle), np.sin(angle)
    return np.block([[cos, -sin], [sin, cos]])


def paired_table():
    half = LANES // 2
    sample = np.arange(LANES)[:, None]
    even = 2 * np.arange(half)[None, :]
    odd = 1 + 2 * np.arange(half)[None, ::-1]
    step = 2.0 * np.pi / (2 * LANES)
    even_angle, odd_angle = (sample * even) * step, (sample * odd) * step
    table = np.zeros((COLS, COLS))
    table[:LANES, :half] = np.cos(even_angle)
    table[:LANES, LANES : LANES + half] = -np.sin(even_angle)
    table[:LANES, LANES] = np.cos(np.pi * sample[:, 0])
    table[LANES:, half:LANES] = np.cos(odd_angle)
    table[LANES:, LANES + half :] = -np.sin(odd_angle)
    return table


def real_dft(values):
    count = len(values)
    if count == 2:
        return [(values[0] + values[1], None), (values[0] - values[1], None)]
    even, odd = real_dft(values[0::2]), real_dft(values[1::2])
    quarter = count // 4
    out = [None] * (count // 2 + 1)
    out[0] = (even[0][0] + odd[0][0], None)
    out[count // 2] = (even[0][0] - odd[0][0], None)
    out[quarter] = (even[quarter][0], -odd[quarter][0])
    for k in range(1, quarter):
        cos, sin = math.cos(2 * math.pi * k / count), math.sin(2 * math.pi * k / count)
        (er, ei), (dr, di) = even[k], odd[k]
        tr, ti = dr * cos + di * sin, di * cos - dr * sin
        out[k] = (er + tr, ei + ti)
        out[count // 2 - k] = (er - tr, ti - ei)
    return out


def real_idft(bins):
    count = 2 * (len(bins) - 1)
    if count == 2:
        return [bins[0][0] + bins[1][0], bins[0][0] - bins[1][0]]
    quarter = count // 4
    first, last = bins[0][0], bins[count // 2][0]
    even, odd = [(first + last, None)], [(first - last, None)]
    for k in range(1, quarter):
        cos, sin = math.cos(2 * math.pi * k / count), math.sin(2 * math.pi * k / count)
        (ar, ai), (br, bi) = bins[k], bins[count // 2 - k]
        even.append((ar + br, ai - bi))
        dr, di = ar - br, ai + bi
        odd.append((dr * cos - di * sin, dr * sin + di * cos))
    mr, mi = bins[quarter]
    even.append((2.0 * mr, None))
    odd.append((-2.0 * mi, None))
    out = [None] * count
    out[0::2] = real_idft(even)
    out[1::2] = real_idft(odd)
    return out


def parts_of(value):
    high = value.astype(BF)
    return high, (value - high.astype(F32)).astype(BF)


def dot(left, right):
    return jnp.dot(left, right, preferred_element_type=F32)


def dot_t(left, right):
    return lax.dot_general(left, right, (((1,), (1,)), ((), ())), preferred_element_type=F32)


def forward_kernel(x_ref, tw_ref, full_ref, pair_ref, out_ref, y_ref):
    rows = x_ref.shape[0]
    pieces = out_ref.shape[1]
    width = COLS // pieces

    def group(i, carry):
        span = pl.ds(pl.multiple_of(i * 8, 8), 8)
        for half in range(2):
            at = slice(128 * half, 128 * half + 128)
            to = slice(LANES + 128 * half, LANES + 128 * half + 128)
            values = [
                x_ref[span, LANES * a + 128 * half : LANES * a + 128 * half + 128]
                for a in range(RADIX)
            ]
            bins = real_dft(values)
            y_ref[0, span, at] = bins[0][0]
            y_ref[0, span, to] = bins[SLOTS][0]
            for k in range(1, SLOTS):
                cos, sin = tw_ref[k : k + 1, at], tw_ref[SLOTS + k : SLOTS + k + 1, at]
                re, im = bins[k]
                y_ref[k, span, at] = re * cos + im * sin
                y_ref[k, span, to] = im * cos - re * sin
        return carry

    lax.fori_loop(0, rows // 8, group, 0)

    def put(first, slots, value):
        value = value.astype(BF)
        for piece in range(pieces):
            part = value[:, width * piece : width * (piece + 1)]
            out_ref[pl.ds(first, slots), piece] = part.reshape(slots, rows, width)

    def product(first, slots, table):
        high, low = parts_of(y_ref[pl.ds(first, slots)].reshape(slots * rows, COLS))
        put(first, slots, dot(high, table[0]) + dot(low, table[0]) + dot(high, table[1]))

    product(0, 1, pair_ref)

    def batch(g, carry):
        product(1 + 5 * g, 5, full_ref)
        return carry

    lax.fori_loop(0, 3, batch, 0)


def forward(x, tw, full, pair, pieces):
    rows, samples = x.shape
    tile = 64
    return pl.pallas_call(
        forward_kernel,
        grid=(rows // tile,),
        in_specs=[
            pl.BlockSpec((tile, samples), lambda i: (i, 0)),
            pl.BlockSpec(tw.shape, lambda i: (0, 0)),
            pl.BlockSpec(full.shape, lambda i: (0, 0, 0)),
            pl.BlockSpec(pair.shape, lambda i: (0, 0, 0)),
        ],
        out_specs=pl.BlockSpec((SLOTS, pieces, tile, COLS // pieces), lambda i: (0, 0, i, 0)),
        out_shape=jax.ShapeDtypeStruct((SLOTS, pieces, rows, COLS // pieces), BF),
        scratch_shapes=[pltpu.VMEM((SLOTS, tile, COLS), F32)],
        compiler_params=pltpu.CompilerParams(vmem_limit_bytes=56 << 20),
        name="time_forward",
    )(x, tw, full, pair)


def channel_kernel(z_ref, bound_ref, tab_ref, full_ref, pair_ref, pair_t_ref, out_ref, y_ref, tw_ref):
    peers = z_ref.shape[0]
    slots = peers // 2
    scale = 1.0 / (peers * LANES)

    @pl.when(pl.program_id(0) == 0)
    def _():
        for k in range(1, slots):
            tw_ref[k] = jnp.broadcast_to(tab_ref[:, k : k + 1], (LANES, 128))
            tw_ref[slots + k] = jnp.broadcast_to(tab_ref[:, 64 + k : 65 + k], (LANES, 128))

    def spans(i):
        low = pl.multiple_of(i * 16, 16)
        return pl.ds(low, 16), pl.ds(pl.multiple_of(LANES + low, 16), 16)

    def before(i, carry):
        span, span_im = spans(i)
        bins = real_dft([z_ref[d, span, :].astype(F32) for d in range(peers)])
        y_ref[span, 0:128] = bins[0][0]
        y_ref[span_im, 0:128] = bins[slots][0]
        for k in range(1, slots):
            cos, sin = tw_ref[k, span, :], tw_ref[slots + k, span, :]
            re, im = bins[k]
            y_ref[span, 128 * k : 128 * k + 128] = re * cos + im * sin
            y_ref[span_im, 128 * k : 128 * k + 128] = re * sin - im * cos
        return carry

    lax.fori_loop(0, LANES // 16, before, 0)
    bound = bound_ref[...]

    def product(table, value):
        high, low = parts_of(value)
        return dot(table[0], high) + dot(table[0], low) + dot(table[1], high)

    row = lax.broadcasted_iota(jnp.int32, (COLS, 128), 0)
    inner = row & (LANES - 1)
    reach = jnp.where(inner < LANES // 2, peers * inner, peers // 2 + peers * (LANES - 1 - inner))
    reach = jnp.where(row == LANES, peers * (LANES // 2), reach)
    gain = jnp.where((row == 0) | (row == LANES), scale, 2.0 * scale)
    spec = product(pair_t_ref, y_ref[:, 0:128])
    spec = jnp.where(reach <= bound, spec * gain, 0.0)
    y_ref[:, 0:128] = product(pair_ref, spec)

    def filtered(first, width):
        at = pl.ds(pl.multiple_of(first * 128, 128), width)
        spec = product(full_ref, y_ref[:, at])
        inner = lax.broadcasted_iota(jnp.int32, (LANES, width), 0)
        lane = lax.broadcasted_iota(jnp.int32, (LANES, width), 1)
        k1 = first + lane // 128
        reach = jnp.where(inner < LANES // 2, k1 + peers * inner, peers * (LANES - inner) - k1)
        wide = bound if width == 128 else jnp.concatenate([bound] * (width // 128), axis=1)
        keep = reach <= wide
        spec = jnp.concatenate(
            [jnp.where(keep, spec[:LANES], 0.0), jnp.where(keep, -spec[LANES:], 0.0)], axis=0
        )
        y_ref[:, at] = product(full_ref, spec)

    def pairs(j, carry):
        filtered(1 + 2 * j, 256)
        return carry

    lax.fori_loop(0, slots // 2 - 1, pairs, 0)
    filtered(slots - 1, 128)

    def after(i, carry):
        span, span_im = spans(i)
        bins = [(y_ref[span, 0:128], None)]
        for k in range(1, slots):
            cos, sin = tw_ref[k, span, :] * scale, tw_ref[slots + k, span, :] * scale
            re, im = y_ref[span, 128 * k : 128 * k + 128], y_ref[span_im, 128 * k : 128 * k + 128]
            bins.append((re * cos - im * sin, re * sin + im * cos))
        bins.append((y_ref[span_im, 0:128], None))
        for d, value in enumerate(real_idft(bins)):
            out_ref[d, span, :] = value.astype(BF)
        return carry

    lax.fori_loop(0, LANES // 16, after, 0)


def channel_filter(z, bound, tab, full, pair, pair_t):
    peers, rows, width = z.shape
    const3 = lambda i: (0, 0, 0)
    return pl.pallas_call(
        channel_kernel,
        grid=(width // 128,),
        in_specs=[
            pl.BlockSpec((peers, rows, 128), lambda i: (0, 0, i)),
            pl.BlockSpec((1, 128), lambda i: (0, i)),
            pl.BlockSpec(tab.shape, lambda i: (0, 0)),
            pl.BlockSpec(full.shape, const3),
            pl.BlockSpec(pair.shape, const3),
            pl.BlockSpec(pair_t.shape, const3),
        ],
        out_specs=pl.BlockSpec((peers, rows, 128), lambda i: (0, 0, i)),
        out_shape=jax.ShapeDtypeStruct(z.shape, BF),
        scratch_shapes=[
            pltpu.VMEM((COLS, peers // 2 * 128), F32),
            pltpu.VMEM((peers, LANES, 128), F32),
        ],
        compiler_params=pltpu.CompilerParams(vmem_limit_bytes=56 << 20),
        name="channel_filter",
    )(z, bound, tab, full, pair, pair_t)


def inverse_kernel(z_ref, tw_ref, full_ref, pair_ref, out_ref, v_ref):
    pieces, rows = z_ref.shape[1], z_ref.shape[2]
    width = COLS // pieces
    scale = 1.0 / (RADIX * LANES)

    def product(first, slots, table, gain):
        total = None
        for piece in range(pieces):
            at = slice(width * piece, width * (piece + 1))
            value = z_ref[pl.ds(first, slots), piece].reshape(slots * rows, width)
            if gain is not None:
                value = value * gain[:, at]
            for level in range(2):
                term = dot_t(value, table[level, :, at])
                total = term if total is None else total + term
        v_ref[pl.ds(first, slots)] = total.reshape(slots, rows, COLS)

    lane = lax.broadcasted_iota(jnp.int32, (1, COLS), 1)
    gain = jnp.where((lane == 0) | (lane == LANES), scale, 2.0 * scale).astype(BF)
    product(0, 1, pair_ref, gain)

    def batch(g, carry):
        product(1 + 5 * g, 5, full_ref, None)
        return carry

    lax.fori_loop(0, 3, batch, 0)

    def group(i, carry):
        span = pl.ds(pl.multiple_of(i * 8, 8), 8)
        for half in range(2):
            at = slice(128 * half, 128 * half + 128)
            to = slice(LANES + 128 * half, LANES + 128 * half + 128)
            bins = [(v_ref[0, span, at], None)]
            for k in range(1, SLOTS):
                cos = tw_ref[k : k + 1, at] * scale
                sin = tw_ref[SLOTS + k : SLOTS + k + 1, at] * scale
                re, im = v_ref[k, span, at], v_ref[k, span, to]
                bins.append((re * cos - im * sin, re * sin + im * cos))
            bins.append((v_ref[0, span, to], None))
            for a, value in enumerate(real_idft(bins)):
                out_ref[span, LANES * a + 128 * half : LANES * a + 128 * half + 128] = value
        return carry

    lax.fori_loop(0, rows // 8, group, 0)


def inverse(z, tw, full, pair):
    slots, pieces, rows, width = z.shape
    samples = RADIX * LANES
    tile = 64
    return pl.pallas_call(
        inverse_kernel,
        grid=(rows // tile,),
        in_specs=[
            pl.BlockSpec((slots, pieces, tile, width), lambda i: (0, 0, i, 0)),
            pl.BlockSpec(tw.shape, lambda i: (0, 0)),
            pl.BlockSpec(full.shape, lambda i: (0, 0, 0)),
            pl.BlockSpec(pair.shape, lambda i: (0, 0, 0)),
        ],
        out_specs=pl.BlockSpec((tile, samples), lambda i: (i, 0)),
        out_shape=jax.ShapeDtypeStruct((rows, samples), F32),
        scratch_shapes=[pltpu.VMEM((SLOTS, tile, COLS), F32)],
        compiler_params=pltpu.CompilerParams(vmem_limit_bytes=56 << 20),
        name="time_inverse",
    )(z, tw, full, pair)


def detect_kernel(before_ref, mid_ref, after_ref, stack_ref, out_ref, sums_ref):
    rows, span = mid_ref.shape
    step = pl.program_id(0)
    block = 512
    tiles = rows // 32
    for b in range(span // block):
        at = slice(block * b, block * (b + 1))
        low = jnp.concatenate(
            [
                before_ref[:, at].astype(F32),
                mid_ref[:, at],
                after_ref[:, at].astype(F32),
                jnp.zeros((64, block), F32),
            ],
            axis=0,
        )
        turned = low.T.astype(BF)
        for j in range(tiles):
            base = j // 4 * 128
            shift = 96 - 32 * (j % 4)
            detection = dot(turned[:, base : base + 256], stack_ref[shift : shift + 256, :])
            squared = (detection * detection).reshape(block // WIN, WIN, 256)
            first = pl.multiple_of(step * (span // WIN) + b * (block // WIN), 8)
            sums_ref[pl.ds(first, 8), 256 * j : 256 * j + 256] = jnp.sum(squared, axis=1)

    @pl.when(step == pl.num_programs(0) - 1)
    def _():
        out_ref[...] = sums_ref[...].T * (1.0 / WIN)


def detect(before, filtered, after, stack, templates):
    rows, samples = filtered.shape
    span = 1024
    windows = samples // WIN
    return pl.pallas_call(
        detect_kernel,
        grid=(samples // span,),
        in_specs=[
            pl.BlockSpec((32, span), lambda i: (0, i)),
            pl.BlockSpec((rows, span), lambda i: (0, i)),
            pl.BlockSpec((32, span), lambda i: (0, i)),
            pl.BlockSpec(stack.shape, lambda i: (0, 0)),
        ],
        out_specs=pl.BlockSpec((rows * templates, windows), lambda i: (0, 0)),
        out_shape=jax.ShapeDtypeStruct((rows * templates, windows), F32),
        scratch_shapes=[pltpu.VMEM((windows, rows * templates), F32)],
        compiler_params=pltpu.CompilerParams(vmem_limit_bytes=56 << 20),
        name="detect",
    )(before, filtered, after, stack)


def bin_bounds(fan_bound):
    by_bin = fan_bound.reshape(LANES // 2, RADIX).T
    falling = by_bin[:, ::-1]
    mirror = jnp.concatenate([falling[SLOTS : SLOTS + 1], falling[:SLOTS:-1]], axis=0)
    real_part = jnp.concatenate([by_bin[:SLOTS], mirror], axis=1)
    bounds = jnp.concatenate([real_part, real_part], axis=1)
    return bounds.at[0, LANES].set(-1)


def stacking(tap_offset, tap_weight):
    span = 2 * HALO + 1
    templates = tap_offset.shape[0]
    offsets_grid = jnp.arange(span, dtype=jnp.int32) - HALO
    matches = (tap_offset[:, :, None] == offsets_grid[None, None, :]).astype(F32)
    kernel_low = jnp.sum(tap_weight[:, :, None] * matches, axis=1).astype(BF)
    period = 257
    line = jnp.pad(kernel_low, ((0, 0), (1, period - 1 - span)))
    band = jnp.tile(line, (1, 32))[:, : 32 * 256].reshape(templates, 32, 256)
    band = jnp.transpose(band, (2, 1, 0)).reshape(256, 32 * templates)
    return jnp.pad(band, ((96, 0), (0, 0)))


def per_device(das_window, fan_bound, tap_offset, tap_weight):
    rows, samples = das_window.shape
    peers = lax.axis_size("chan")
    pieces = peers // SLOTS
    templates = tap_offset.shape[0]
    me = lax.axis_index("chan")
    full = jnp.asarray(split_table(full_table()))
    pair_np = split_table(paired_table())
    pair = jnp.asarray(pair_np)
    pair_t = jnp.asarray(np.ascontiguousarray(np.swapaxes(pair_np, 1, 2)))
    order = np.arange(SLOTS)[:, None] * np.arange(LANES)[None, :]
    angle = 2.0 * np.pi * order / samples
    tw = jnp.asarray(np.concatenate([np.cos(angle), np.sin(angle)]).astype(np.float32))
    tab_np = np.zeros((LANES, 128), np.float32)
    order = np.arange(LANES)[:, None] * np.arange(peers // 2)[None, :]
    angle = 2.0 * np.pi * order / (peers * LANES)
    tab_np[:, : peers // 2] = np.cos(angle)
    tab_np[:, 64 : 64 + peers // 2] = np.sin(angle)
    tab = jnp.asarray(tab_np)

    width = COLS // pieces
    bounds = bin_bounds(fan_bound).reshape(peers, width)
    bound = lax.dynamic_slice_in_dim(bounds, me, 1, 0)
    stack = stacking(tap_offset, tap_weight)

    spectrum = forward(das_window, tw, full, pair, pieces)
    sent = spectrum.reshape(peers, rows, width)
    by_freq = lax.all_to_all(sent, "chan", split_axis=0, concat_axis=0, tiled=True)
    wave = channel_filter(by_freq, bound, tab, full, pair, pair_t)
    back = lax.all_to_all(wave, "chan", split_axis=0, concat_axis=0, tiled=True)
    filtered = inverse(back.reshape(SLOTS, pieces, rows, width), tw, full, pair)

    up = [(i, i + 1) for i in range(peers - 1)]
    down = [(i + 1, i) for i in range(peers - 1)]
    before = lax.ppermute(filtered[rows - 32 :].astype(BF), "chan", up)
    after = lax.ppermute(filtered[:32].astype(BF), "chan", down)
    energy = detect(before, filtered, after, stack, templates)
    return filtered, energy.reshape(rows, templates, samples // WIN)


def solution(mesh):
    return jax.shard_map(
        per_device,
        mesh=mesh,
        in_specs=(P(("survey", "chan"), None), P(), P(), P()),
        out_specs=(P(("survey", "chan"), None), P(("survey", "chan"), None, None)),
        check_vma=False,
    )
```

time: 750 us -> 311 us (0.41); the launches traced: 741 us -> 310 us
  waiting for transfers between devices: 344 us -> 96.6 us
  matrix products: 184 us -> 0 us
  local copies, waits for them, and re-layouts: 120 us -> 6.8 us
  blocking collectives: 0 us -> 97.2 us
  Pallas kernels: 0 us -> 91.3 us
  other arithmetic: 67 us -> 4.76 us
  loops' own time: 7.54 us -> 0 us
    all_to_all x2 -> x1, waiting for transfers between devices: 333 us -> 85.6 us  [per_device(): lax.all_to_all(sent, 'chan', split_axis=0, concat_axis=0, tiled=True)]
    dot_general x13 -> x0, matrix products: 184 us -> none  [the longest x2 44.2 us: channel_transform(): out = jnp.einsum('kbpn,pkbqm->mkqn', first, second_table, precision=PRECISE)]
    all_to_all x0 -> x1, blocking collectives: none -> 97.2 us  [per_device(): back = lax.all_to_all(wave, 'chan', split_axis=0, concat_axis=0, tiled=True)]
    pallas_call x0 -> x4, Pallas kernels: none -> 91.3 us  [the longest x1 46.7 us: channel_filter(): pl.pallas_call(channel_kernel, grid=(width // 128,), in_specs=[pl.BlockSp...]
    all_to_all x4 -> x0, local copies, waits for them, and re-layouts: 32.3 us -> none  [the longest x2 16.2 us: per_device(): lax.all_to_all(spectrum, 'chan', split_axis=2, concat_axis=0, tiled=True)]
    div x6 -> x0, local copies, waits for them, and re-layouts: 28.8 us -> none  [the longest x2 28.3 us: per_device(): back = channel_transform(wave * passing[:, None, :], 1.0) / channel_count]
    reshape x1 -> x3, local copies, waits for them, and re-layouts: 23.4 us -> 0.23 us  [the longest x2 0.13 us: bin_bounds(): by_bin = fan_bound.reshape(LANES // 2, RADIX).T]
    transpose x2 -> x1, local copies, waits for them, and re-layouts: 21.7 us -> 0.08 us  [stacking(): band = jnp.transpose(band, (2, 1, 0)).reshape(256, 32 * templates)]
  transfers between devices with their start and end apart: 4 -> 3, of which waited for: 4 -> 3; matrix products, arithmetic and copies ran while one was open for 4% -> 2% of each run, Pallas kernels for 0% -> 0%
where the time goes in v1:
time: 311 us; the launch traced here: 310 us
  blocking collectives  97.2 us (31%)
  waiting for transfers between devices  96.6 us (31%)
  Pallas kernels  91.3 us (29%)
  starting transfers between devices  11.5 us (4%)
  local copies, waits for them, and re-layouts  6.8 us (2%)
  other arithmetic  4.76 us (2%)
    all_to_all x1, blocking collectives, per_device(): back = lax.all_to_all(wave, 'chan', split_axis=0, concat_axis=0, tiled=True)  97.2 us
    all_to_all x1, waiting for transfers between devices, per_device(): lax.all_to_all(sent, 'chan', split_axis=0, concat_axis=0, tiled=True)  85.6 us
    pallas_call x1, Pallas kernels, channel_filter(): pl.pallas_call(channel_kernel, grid=(width // 128,), in_specs=[pl.BlockSp...  46.7 us
    pallas_call x1, Pallas kernels, forward(): pl.pallas_call(forward_kernel, grid=(rows // tile,), in_specs=[pl.BlockSp...  16 us
    pallas_call x1, Pallas kernels, inverse(): pl.pallas_call(inverse_kernel, grid=(rows // tile,), in_specs=[pl.BlockSp...  15 us
    pallas_call x1, Pallas kernels, detect(): pl.pallas_call(detect_kernel, grid=(samples // span,), in_specs=[pl.Block...  13.6 us
    ppermute x1, waiting for transfers between devices, per_device(): before = lax.ppermute(filtered[rows - 32:].astype(BF), 'chan', up)  7.41 us
    all_to_all x1, starting transfers between devices, per_device(): lax.all_to_all(sent, 'chan', split_axis=0, concat_axis=0, tiled=True)  6.63 us
  transfers between devices with their start and end apart: 3, of which 3 were waited for; matrix products, arithmetic and copies ran while one was open for 2% of the time, Pallas kernels for 0%

profile of v1, /device:TPU:17, one launch (start us, length us, event | category | flops | bytes accessed | tf_op | source)
XLA Modules:
  0.0 310.2 jit_solution(10468127429703377674)
XLA Ops:
  0.6 16.0 %time_forward.1 = bf16[16,1,256,512]{3,2,1,0:T(8,128)(2,1)} custom-call(f32[256,8192]{1,0:T(8,128)} %x_ref.1, f32[32,256]{1,0:T(8,128)} %constant.55.clone.tw_ref, bf16[2,512,512]{2,1,0:T(8,128)(2,1)} %constant.52.clone.full_ref, bf16[2,512,512]{2,1,0:T(8,128)(2,1)} %constant.53.clone.pair_ref), custom_call_target="tpu_custom_call" | custom-call | tf_op jit(solution)/shard_map/time_forward/pallas_call | solution.py:154
  16.6 0.0 copy-start.2
  16.6 0.0 copy-start.5
  16.6 6.6 %all-to-all-start = ((bf16[16,256,512]{2,1,0:T(8,128)(2,1)}), bf16[16,256,512]{2,1,0:T(8,128)(2,1)}, u32[]{:S(2)}, u32[]{:S(2)}) async-start(bf16[16,256,512]{2,1,0:T(8,128)(2,1)} %bitcast.17), calls=%async_computation | async-start | bytes 8388608 | tf_op jit(solution)/shard_map/all_to_all | solution.py:442
  23.3 0.0 copy-done.2
  23.3 0.1 reshape.70
  23.4 0.1 copy.14
  23.5 0.1 rev.4
  23.5 0.1 slice.48
  23.6 0.6 fusion.1
  24.2 1.8 dynamic-slice.9
  26.1 0.0 copy-done.5
  26.1 0.6 and_reduce_fusion
  28.0 1.3 scatter.4
  29.3 0.6 constant_dynamic-slice_fusion.bound_ref
  29.9 85.6 %all-to-all-done.z_ref = bf16[16,256,512]{2,1,0:T(8,128)(2,1)} async-done(((bf16[16,256,512]{2,1,0:T(8,128)(2,1)}), bf16[16,256,512]{2,1,0:T(8,128)(2,1)}, u32[]{:S(2)}, u32[]{:S(2)}) %all-to-all-start) | async-done | bytes 4194336 | tf_op jit(solution)/shard_map/all_to_all | solution.py:442
  115.5 46.7 %channel_filter.1 = bf16[16,256,512]{2,1,0:T(8,128)(2,1)} custom-call(bf16[16,256,512]{2,1,0:T(8,128)(2,1)} %all-to-all-done.z_ref, s32[1,512]{1,0:T(1,128)} %constant_dynamic-slice_fusion.bound_ref, f32[256,128]{1,0:T(8,128)} %constant.56.clone.tab_ref, bf16[2,512,512]{2,1,0:T(8,128)(2,1)} %constant.52.clone.full_ref, ...), custom_call_target="tpu_custom_call" | custom-call | tf_op jit(solution)/shard_map/channel_filter/pallas_call | solution.py:253
  162.2 97.2 %all_to_all.10 = bf16[16,256,512]{2,1,0:T(8,128)(2,1)} all-to-all(bf16[16,256,512]{2,1,0:T(8,128)(2,1)} %channel_filter.1), channel_id=1, replica_groups=mesh['survey'=2,'chan'=16] {'chan'}, dimensions={0} | all-to-all | bytes 8388608 | tf_op jit(solution)/shard_map/all_to_all | solution.py:444
  259.4 15.0 %time_inverse.1.mid_ref = f32[256,8192]{1,0:T(8,128)} custom-call(bf16[16,1,256,512]{3,2,1,0:T(8,128)(2,1)} %bitcast.18, f32[32,256]{1,0:T(8,128)} %constant.55.clone.tw_ref, bf16[2,512,512]{2,1,0:T(8,128)(2,1)} %constant.52.clone.full_ref, bf16[2,512,512]{2,1,0:T(8,128)(2,1)} %constant.53.clone.pair_ref), custom_call_target="tpu_custom_call" | custom-call | tf_op jit(solution)/shard_map/time_inverse/pallas_call | solution.py:325
  274.3 0.0 copy-start.3
  274.3 0.0 copy-start.4
  274.3 4.0 %convert.4 = bf16[256,8192]{1,0:T(8,128)(2,1)S(1)} convert(f32[256,8192]{1,0:T(8,128)} %time_inverse.1.mid_ref) | non-fusion elementwise | flops 2097152 | bytes 12582912 | tf_op jit(solution)/shard_map/convert.1
  278.3 0.1 fusion
  278.4 2.1 collective-permute-start
  280.5 2.8 collective-permute-start.1
  283.3 0.0 copy-done.3
  283.3 0.0 copy-done.4
  283.3 0.1 select_reduce_fusion
  283.5 0.1 pad.12
  283.6 0.3 tile.10
  283.9 0.1 copy.21
  284.0 0.1 copy.16
  284.1 0.7 pad.13.stack_ref
  284.8 7.4 %collective-permute-done.before_ref = bf16[32,8192]{1,0:T(8,128)(2,1)S(1)} collective-permute-done((bf16[32,8192]{1,0:T(8,128)(2,1)S(1)}, bf16[32,8192]{1,0:T(8,128)(2,1)S(1)}, u32[]{:S(2)}, u32[]{:S(2)}) %collective-permute-start) | collective-permute-done | bytes 524320 | tf_op jit(solution)/shard_map/ppermute | solution.py:449
  292.2 0.0 copy-start
  292.2 3.6 %collective-permute-done.1.after_ref = bf16[32,8192]{1,0:T(8,128)(2,1)S(1)} collective-permute-done((bf16[32,8192]{1,0:T(8,128)(2,1)S(1)}, bf16[32,8192]{1,0:T(8,128)(2,1)S(1)}, u32[]{:S(2)}, u32[]{:S(2)}) %collective-permute-start.1) | collective-permute-done | bytes 524320 | tf_op jit(solution)/shard_map/ppermute | solution.py:450
  295.8 0.0 copy-done
  295.8 0.0 copy-start.1
  295.8 0.8 copy-done.1
  296.6 13.6 %detect.1 = f32[2048,128]{1,0:T(8,128)} custom-call(bf16[32,8192]{1,0:T(8,128)(2,1)} %copy-done, f32[256,8192]{1,0:T(8,128)} %time_inverse.1.mid_ref, bf16[32,8192]{1,0:T(8,128)(2,1)} %copy-done.1, bf16[352,256]{1,0:T(8,128)(2,1)} %pad.13.stack_ref), custom_call_target="tpu_custom_call" | custom-call | tf_op jit(solution)/shard_map/detect/pallas_call | solution.py:376
  (9 shorter events, 0.1 us)
Async XLA Ops:
  16.6 6.6 %copy-start.2 = (s32[4096]{0:T(1024)S(1)}, s32[4096]{0:T(1024)}, u32[]{:S(2)}) copy-start(s32[4096]{0:T(1024)} %param.12) | copy-start | bytes 49156
  16.6 9.4 %copy-start.5 = (s32[2]{0:T(128)S(1)}, s32[2]{0:T(128)}, u32[]{:S(2)}) copy-start(s32[2]{0:T(128)} %constant.44.clone.1) | copy-start | bytes 28
  16.6 98.8 %all-to-all-start = ((bf16[16,256,512]{2,1,0:T(8,128)(2,1)}), bf16[16,256,512]{2,1,0:T(8,128)(2,1)}, u32[]{:S(2)}, u32[]{:S(2)}) async-start(bf16[16,256,512]{2,1,0:T(8,128)(2,1)} %bitcast.17), calls=%async_computation | async-start | bytes 8388608 | tf_op jit(solution)/shard_map/all_to_all | solution.py:442
  274.3 9.0 %copy-start.3 = (f32[8,32]{1,0:T(8,128)S(1)}, f32[8,32]{1,0:T(8,128)}, u32[]{:S(2)}) copy-start(f32[8,32]{1,0:T(8,128)} %param.14) | copy-start | bytes 3076
  274.3 9.0 %copy-start.4 = (s32[8,32]{1,0:T(8,128)S(1)}, s32[8,32]{1,0:T(8,128)}, u32[]{:S(2)}) copy-start(s32[8,32]{1,0:T(8,128)} %param.13) | copy-start | bytes 3076
  278.4 13.8 %collective-permute-start = (bf16[32,8192]{1,0:T(8,128)(2,1)S(1)}, bf16[32,8192]{1,0:T(8,128)(2,1)S(1)}, u32[]{:S(2)}, u32[]{:S(2)}) collective-permute-start(bf16[32,8192]{1,0:T(8,128)(2,1)S(1)} %get-tuple-element.15), channel_id=1, source_target_pairs={{0,1},{1,2},{2,3},{3,4},{4,5},{5,6},{6,7},{7,8},{8,9},{9,10},{10,1... | collective-permute-start | bytes 1572872 | tf_op jit(solution)/shard_map/ppermute | solution.py:449
  280.5 15.3 %collective-permute-start.1 = (bf16[32,8192]{1,0:T(8,128)(2,1)S(1)}, bf16[32,8192]{1,0:T(8,128)(2,1)S(1)}, u32[]{:S(2)}, u32[]{:S(2)}) collective-permute-start(bf16[32,8192]{1,0:T(8,128)(2,1)S(1)} %get-tuple-element.14), channel_id=1, source_target_pairs={{1,0},{2,1},{3,2},{4,3},{5,4},{6,5},{7,6},{8,7},{9,8},{10,9},{11,1... | collective-permute-start | bytes 1572872 | tf_op jit(solution)/shard_map/ppermute | solution.py:450
  292.2 3.6 %copy-start = (bf16[32,8192]{1,0:T(8,128)(2,1)}, bf16[32,8192]{1,0:T(8,128)(2,1)S(1)}, u32[]{:S(2)}) copy-start(bf16[32,8192]{1,0:T(8,128)(2,1)S(1)} %collective-permute-done.before_ref) | copy-start | bytes 1572868
  295.8 0.8 copy-start.1
